TPU v7x, 32 devices: a whole 2x2x4 slice. The times are simulated.
32 devices in a mesh: wide: 8 (over z, x), narrow: 4 (over y, core).
Axes of the slice: x: 2, y: 2, z: 4, core: 2. Of those that a mesh axis runs over, the one named last changes fastest.
Arguments:
- patches: bfloat16 [4096, 256], P(('wide', 'narrow')), may hold values from -6 to 6
- token_kind: int32 [4096], P(('wide', 'narrow')), may hold values 0 or 1
- mask_slots: int32 [16, 64], P('wide'), may hold values from 0 to 255
- projector: bfloat16 [2, 256, 768], replicated, may hold values from -0.375 to 0.375
- offsets: bfloat16 [2, 768], replicated, may hold values from -3 to 3
- placeholder: bfloat16 [768], replicated, may hold values from -4 to 4
- positions: bfloat16 [256, 768], replicated, may hold values from -3 to 3
- scales: bfloat16 [2, 2, 768], replicated, may hold values from 0.5 to 1.5
- shifts: bfloat16 [2, 2, 768], replicated, may hold values from -3 to 3
- attention: bfloat16 [2, 3, 768, 768], P(None, None, None, 'narrow'), may hold values from -0.21875 to 0.21875
- attn_bias: bfloat16 [2, 2, 768], P(None, None, 'narrow'), may hold values from -3 to 3
- combiner: bfloat16 [2, 768, 768], P(None, 'narrow'), may hold values from -1.75 to 1.75
- comb_bias: bfloat16 [2, 768], replicated, may hold values from -3 to 3
- expander: bfloat16 [2, 768, 3072], P(None, None, 'narrow'), may hold values from -0.21875 to 0.21875
- expand_bias: bfloat16 [2, 3072], P(None, 'narrow'), may hold values from -3 to 3
- reducer: bfloat16 [2, 3072, 768], P(None, 'narrow'), may hold values from -0.15625 to 0.15625
- reduce_bias: bfloat16 [2, 768], replicated, may hold values from -3 to 3
- cotangent: bfloat16 [4096, 768], P(('wide', 'narrow')), may hold values from -6 to 6
Outputs:
- encoded: float32 [4096, 768], P(('wide', 'narrow'))
- grad_patches: float32 [4096, 256], P(('wide', 'narrow'))
- grad_projector: float32 [2, 256, 768], replicated
- grad_offsets: float32 [2, 768], replicated
- grad_placeholder: float32 [768], replicated
- grad_positions: float32 [256, 768], replicated
- grad_scales: float32 [2, 2, 768], replicated
- grad_shifts: float32 [2, 2, 768], replicated
- grad_attention: float32 [2, 3, 768, 768], P(None, None, None, 'narrow')
- grad_attnbias: float32 [2, 2, 768], P(None, None, 'narrow')
- grad_combiner: float32 [2, 768, 768], P(None, 'narrow')
- grad_combbias: float32 [2, 768], replicated
- grad_expander: float32 [2, 768, 3072], P(None, None, 'narrow')
- grad_expbias: float32 [2, 3072], P(None, 'narrow')
- grad_reducer: float32 [2, 3072, 768], P(None, 'narrow')
- grad_redbias: float32 [2, 768], replicated
Inputs may be any that keep to these rules, and one draw needn't show every extreme that they name: `mask_slots`: positions within the clip; a position may appear more than once.
All inputs are finite; a program needn't handle non-finite values. No bound on the sum of `token_kind` on one device may be relied on, other than what follows from the above.
Results may differ from a plain program's by a relative error of at most 0.025.
Values may be sent and summed in bfloat16 or wider, within the bound.
A program may use at most 128 MiB of HBM per device.

v0:
```python
from functools import partial
import math
import jax
import jax.numpy as jnp
from jax import lax
from jax.sharding import PartitionSpec as P

HD = 64
norm_eps = 1e-06


def normalize(values, gain, shift):
    center = values - jnp.mean(values, axis=-1, keepdims=True)
    variance = jnp.mean(center * center, axis=-1, keepdims=True)
    return center * lax.rsqrt(variance + norm_eps) * gain + shift


def norm_params(values, grad):
    center = values - jnp.mean(values, axis=-1, keepdims=True)
    variance = jnp.mean(center * center, axis=-1, keepdims=True)
    hat = center * lax.rsqrt(variance + norm_eps)
    return (jnp.sum(grad * hat, axis=0), jnp.sum(grad, axis=0))


def share_rows(values):
    return lax.all_gather(values, "narrow", axis=0, tiled=True)


def share_grads(values):
    return lax.all_gather(values, "narrow", axis=0, tiled=True)


def sum_forward(source, weight, local_rows):

    def term(start, count):
        return jnp.dot(source, weight, preferred_element_type=jnp.float32)

    return lax.psum_scatter(
        term(jnp.int32(0), local_rows * lax.axis_size("narrow")).astype(jnp.bfloat16),
        "narrow",
        scatter_dimension=0,
        tiled=True,
    ).astype(jnp.float32)


def sum_backward(source, weight, local_rows):

    def term(start, count):
        return jnp.einsum("rk,dk->rd", source, weight, preferred_element_type=jnp.float32)

    return lax.psum_scatter(
        term(jnp.int32(0), local_rows * lax.axis_size("narrow")).astype(jnp.bfloat16),
        "narrow",
        scatter_dimension=0,
        tiled=True,
    ).astype(jnp.float32)


def attend_block(inputs):
    query, key, value = inputs
    scores = jnp.einsum("bqhd,bkhd->bhqk", query, key, preferred_element_type=jnp.float32)
    top = jnp.max(scores, axis=-1, keepdims=True)
    raised = jnp.exp(scores - top)
    total = jnp.sum(raised, axis=-1, keepdims=True)
    weights = raised / total
    mixed = jnp.einsum(
        "bhqk,bkhd->bqhd", weights.astype(jnp.bfloat16), value, preferred_element_type=jnp.float32
    )
    return (mixed.astype(jnp.bfloat16), top + jnp.log(total))


def attend_back(inputs):
    query, key, value, log_total, grad_mixed = inputs
    scores = jnp.einsum("bqhd,bkhd->bhqk", query, key, preferred_element_type=jnp.float32)
    weights = jnp.exp(scores - log_total)
    grad_weights = jnp.einsum(
        "bqhd,bkhd->bhqk", grad_mixed, value, preferred_element_type=jnp.float32
    )
    grad_value = jnp.einsum(
        "bhqk,bqhd->bkhd",
        weights.astype(jnp.bfloat16),
        grad_mixed,
        preferred_element_type=jnp.float32,
    ).astype(jnp.bfloat16)
    center = jnp.sum(weights * grad_weights, axis=-1, keepdims=True)
    grad_scores = (weights * (grad_weights - center)).astype(jnp.bfloat16)
    grad_query = jnp.einsum(
        "bhqk,bkhd->bqhd", grad_scores, key, preferred_element_type=jnp.float32
    ).astype(jnp.bfloat16)
    grad_key = jnp.einsum(
        "bhqk,bqhd->bkhd", grad_scores, query, preferred_element_type=jnp.float32
    ).astype(jnp.bfloat16)
    return (grad_query, grad_key, grad_value)


def per_device(
    patches,
    token_kind,
    mask_slots,
    projector,
    offsets,
    placeholder,
    positions,
    scales,
    shifts,
    attention,
    attn_bias,
    combiner,
    comb_bias,
    expander,
    expand_bias,
    reducer,
    reduce_bias,
    cotangent,
):
    local_rows, patch_len = patches.shape
    width = projector.shape[2]
    clip_count = mask_slots.shape[0]
    seq_len = positions.shape[0]
    group_rows = clip_count * seq_len
    start_row = lax.axis_index("narrow") * local_rows
    head_cols = attention.shape[3]
    local_heads = head_cols // HD
    layer_count = scales.shape[0]
    scale = HD ** (-0.5)
    block_clips = math.gcd(clip_count, max(1, 512 // seq_len))
    block_count = clip_count // block_clips
    head_shape = (block_count, block_clips, seq_len, local_heads, HD)
    place = jnp.arange(seq_len, dtype=jnp.int32)
    masked_group = jnp.any(mask_slots[:, :, None] == place[None, None, :], axis=1).reshape(
        group_rows, 1
    )
    masked = lax.dynamic_slice_in_dim(masked_group, start_row, local_rows, 0)
    is_patch = (token_kind == 1).reshape(local_rows, 1)
    blank = jnp.zeros_like(patches)
    widened = jnp.concatenate(
        [jnp.where(is_patch, blank, patches), jnp.where(is_patch, patches, blank)], axis=1
    )
    flat_projector = projector.reshape(2 * patch_len, width)
    lifted = jnp.dot(widened, flat_projector, preferred_element_type=jnp.float32)
    shifted = lifted + jnp.where(
        is_patch, offsets[1].astype(jnp.float32), offsets[0].astype(jnp.float32)
    )
    table = jnp.broadcast_to(positions.astype(jnp.float32)[None], (clip_count, seq_len, width))
    position_rows = lax.dynamic_slice_in_dim(
        table.reshape(group_rows, width), start_row, local_rows, 0
    )
    stream = jnp.where(masked, placeholder.astype(jnp.float32), shifted) + position_rows
    grad_top = cotangent.astype(jnp.float32)
    saved = []
    for layer in range(layer_count):
        first = normalize(
            stream, scales[layer, 0].astype(jnp.float32), shifts[layer, 0].astype(jnp.float32)
        ).astype(jnp.bfloat16)
        first_all = share_rows(first)
        joined = attention[layer].transpose(1, 0, 2).reshape(width, 3 * head_cols)
        triple = jnp.dot(first_all, joined, preferred_element_type=jnp.float32)
        query = ((triple[:, :head_cols] + attn_bias[layer, 0].astype(jnp.float32)) * scale).astype(
            jnp.bfloat16
        )
        key = triple[:, head_cols : 2 * head_cols].astype(jnp.bfloat16)
        value = (triple[:, 2 * head_cols :] + attn_bias[layer, 1].astype(jnp.float32)).astype(
            jnp.bfloat16
        )
        mixed, log_total = lax.map(
            attend_block,
            (query.reshape(head_shape), key.reshape(head_shape), value.reshape(head_shape)),
        )
        mixed = mixed.reshape(group_rows, head_cols)
        middle = (
            stream
            + sum_forward(mixed, combiner[layer], local_rows)
            + comb_bias[layer].astype(jnp.float32)
        )
        second = normalize(
            middle, scales[layer, 1].astype(jnp.float32), shifts[layer, 1].astype(jnp.float32)
        ).astype(jnp.bfloat16)
        second_all = share_rows(second)
        pre_act = jnp.dot(
            second_all, expander[layer], preferred_element_type=jnp.float32
        ) + expand_bias[layer].astype(jnp.float32)
        hidden = jax.nn.gelu(pre_act, approximate=False).astype(jnp.bfloat16)
        saved.append(
            (
                stream,
                first_all,
                query,
                key,
                value,
                log_total,
                mixed,
                middle,
                second_all,
                pre_act,
                hidden,
            )
        )
        stream = (
            middle
            + sum_forward(hidden, reducer[layer], local_rows)
            + reduce_bias[layer].astype(jnp.float32)
        )
    grad_stream = grad_top
    owned = [None] * layer_count
    gain_grads = [None] * layer_count
    shift_grads = [None] * layer_count
    comb_grads = [None] * layer_count
    red_grads = [None] * layer_count
    for layer in reversed(range(layer_count)):
        (
            stream_in,
            first_all,
            query,
            key,
            value,
            log_total,
            mixed,
            middle,
            second_all,
            pre_act,
            hidden,
        ) = saved[layer]
        red_grads[layer] = jnp.sum(grad_stream, axis=0)
        out_round = share_grads(grad_stream.astype(jnp.bfloat16))
        grad_reducer = jnp.einsum(
            "rf,rd->fd", hidden, out_round, preferred_element_type=jnp.float32
        )
        grad_hidden = jnp.einsum(
            "rd,fd->rf", out_round, reducer[layer], preferred_element_type=jnp.float32
        )
        _, gelu_back = jax.vjp(partial(jax.nn.gelu, approximate=False), pre_act)
        grad_pre = gelu_back(grad_hidden)[0]
        grad_expbias = jnp.sum(grad_pre, axis=0)
        pre_round = grad_pre.astype(jnp.bfloat16)
        grad_expander = jnp.einsum(
            "rd,rf->df", second_all, pre_round, preferred_element_type=jnp.float32
        )
        grad_second = sum_backward(pre_round, expander[layer], local_rows)
        _, norm_back = jax.vjp(
            normalize,
            middle,
            scales[layer, 1].astype(jnp.float32),
            shifts[layer, 1].astype(jnp.float32),
        )
        grad_mid_in = norm_back(grad_second)[0]
        grad_gain_two, grad_shift_two = norm_params(middle, grad_second)
        grad_middle = grad_stream + grad_mid_in
        comb_grads[layer] = jnp.sum(grad_middle, axis=0)
        mid_round = share_grads(grad_middle.astype(jnp.bfloat16))
        grad_combiner = jnp.einsum(
            "re,rd->ed", mixed, mid_round, preferred_element_type=jnp.float32
        )
        grad_mixed = jnp.einsum(
            "rd,ed->re", mid_round, combiner[layer], preferred_element_type=jnp.float32
        ).astype(jnp.bfloat16)
        grad_query, grad_key, grad_value = lax.map(
            attend_back,
            (
                query.reshape(head_shape),
                key.reshape(head_shape),
                value.reshape(head_shape),
                log_total,
                grad_mixed.reshape(head_shape),
            ),
        )
        grad_query = grad_query.reshape(group_rows, head_cols) * scale
        grad_value = grad_value.reshape(group_rows, head_cols)
        grad_triple = jnp.concatenate(
            [grad_query, grad_key.reshape(group_rows, head_cols), grad_value], axis=1
        )
        grad_joined = jnp.einsum(
            "rd,rk->dk", first_all, grad_triple, preferred_element_type=jnp.float32
        )
        grad_attention = grad_joined.reshape(width, 3, head_cols).transpose(1, 0, 2)
        grad_attnbias = jnp.stack(
            [
                jnp.sum(grad_query.astype(jnp.float32), axis=0),
                jnp.sum(grad_value.astype(jnp.float32), axis=0),
            ]
        )
        joined = attention[layer].transpose(1, 0, 2).reshape(width, 3 * head_cols)
        grad_first = sum_backward(grad_triple, joined, local_rows)
        _, norm_back = jax.vjp(
            normalize,
            stream_in,
            scales[layer, 0].astype(jnp.float32),
            shifts[layer, 0].astype(jnp.float32),
        )
        grad_in = norm_back(grad_first)[0]
        grad_gain_one, grad_shift_one = norm_params(stream_in, grad_first)
        grad_stream = grad_middle + grad_in
        gain_grads[layer] = jnp.stack([grad_gain_one, grad_gain_two])
        shift_grads[layer] = jnp.stack([grad_shift_one, grad_shift_two])
        own_grads = (
            grad_attention,
            grad_attnbias,
            grad_combiner,
            grad_expander,
            grad_expbias,
            grad_reducer,
        )
        own_grads = lax.psum(
            (
                grad_attention,
                grad_attnbias,
                grad_combiner,
                grad_expander,
                grad_expbias,
                grad_reducer,
            ),
            "wide",
        )
        owned[layer] = own_grads
    sum_attention, sum_attnbias, sum_combiner, sum_expander, sum_expbias, sum_reducer = [
        jnp.stack([owned[layer][index] for layer in range(layer_count)]) for index in range(6)
    ]
    spread_rows = lax.dynamic_update_slice_in_dim(
        jnp.zeros((group_rows, width), jnp.float32), grad_stream, start_row, 0
    )
    grad_positions = jnp.sum(spread_rows.reshape(clip_count, seq_len, width), axis=0)
    grad_placeholder = jnp.sum(jnp.where(masked, grad_stream, 0.0), axis=0)
    grad_lifted = jnp.where(masked, 0.0, grad_stream)
    grad_offsets = jnp.stack(
        [
            jnp.sum(jnp.where(is_patch, 0.0, grad_lifted), axis=0),
            jnp.sum(jnp.where(is_patch, grad_lifted, 0.0), axis=0),
        ]
    )
    lifted_round = grad_lifted.astype(jnp.bfloat16)
    grad_projector = jnp.einsum(
        "rp,rd->pd", widened, lifted_round, preferred_element_type=jnp.float32
    ).reshape(2, patch_len, width)
    both_halves = jnp.einsum(
        "rd,pd->rp", lifted_round, flat_projector, preferred_element_type=jnp.float32
    )
    grad_patches = jnp.where(is_patch, both_halves[:, patch_len:], both_halves[:, :patch_len])
    grad_scales = jnp.stack(gain_grads)
    grad_shifts = jnp.stack(shift_grads)
    grad_combbias = jnp.stack(comb_grads)
    grad_redbias = jnp.stack(red_grads)
    (
        grad_scales,
        grad_shifts,
        grad_combbias,
        grad_redbias,
        grad_projector,
        grad_offsets,
        grad_placeholder,
        grad_positions,
    ) = lax.psum(
        (
            grad_scales,
            grad_shifts,
            grad_combbias,
            grad_redbias,
            grad_projector,
            grad_offsets,
            grad_placeholder,
            grad_positions,
        ),
        ("wide", "narrow"),
    )
    return (
        stream,
        grad_patches,
        grad_projector,
        grad_offsets,
        grad_placeholder,
        grad_positions,
        grad_scales,
        grad_shifts,
        sum_attention,
        sum_attnbias,
        sum_combiner,
        grad_combbias,
        sum_expander,
        sum_expbias,
        sum_reducer,
        grad_redbias,
    )


def solution(mesh):
    return jax.shard_map(
        per_device,
        mesh=mesh,
        in_specs=(
            P(("wide", "narrow"), None),
            P(("wide", "narrow")),
            P("wide", None),
            P(),
            P(),
            P(),
            P(),
            P(),
            P(),
            P(None, None, None, "narrow"),
            P(None, None, "narrow"),
            P(None, "narrow", None),
            P(),
            P(None, None, "narrow"),
            P(None, "narrow"),
            P(None, "narrow", None),
            P(),
            P(("wide", "narrow"), None),
        ),
        out_specs=(
            P(("wide", "narrow"), None),
            P(("wide", "narrow"), None),
            P(),
            P(),
            P(),
            P(),
            P(),
            P(),
            P(None, None, None, "narrow"),
            P(None, None, "narrow"),
            P(None, "narrow", None),
            P(),
            P(None, None, "narrow"),
            P(None, "narrow"),
            P(None, "narrow", None),
            P(),
        ),
        check_vma=False,
    )
```

profile of v0, /device:TPU:0, one launch (start us, length us, event | category | flops | bytes accessed | tf_op | source)
XLA Modules:
  0.0 964.3 jit_solution(6585855473328736234)
XLA Ops:
  15.2 10.1 %all_gather.24 = bf16[512,768]{1,0:T(8,128)(2,1)S(1)} all-gather(bf16[128,768]{1,0:T(8,128)(2,1)S(1)} %add_convert_fusion.3), channel_id=1, replica_groups=mesh['wide'=8,'narrow'=4] {'narrow'}, dimensions={0}, use_global_device_ids=true | all-gather | bytes 983040 | tf_op jit(solution)/shard_map/all_gather | solution.py:26
  32.6 23.0 %reduce-scatter.9.cloned.1.call-done = bf16[128,768]{1,0:T(8,128)(2,1)} async-done(((bf16[512,768]{1,0:T(8,128)(2,1)}), bf16[128,768]{1,0:T(8,128)(2,1)}) %reduce-scatter.9.cloned.1.call-update) | async-done | bytes 196624 | tf_op jit(solution)/shard_map/reduce_scatter | solution.py:38
  57.1 8.2 all_gather.25
  65.4 5.4 multiply_convert_fusion.3
  74.1 23.1 %reduce-scatter.11.cloned.1.call-done = bf16[128,768]{1,0:T(8,128)(2,1)} async-done(((bf16[512,768]{1,0:T(8,128)(2,1)}), bf16[128,768]{1,0:T(8,128)(2,1)}) %reduce-scatter.11.cloned.1.call-update) | async-done | bytes 196624 | tf_op jit(solution)/shard_map/reduce_scatter | solution.py:38
  98.8 8.2 all_gather.26
  110.2 1.7 squeeze.116
  112.0 2.0 fusion.70
  122.2 10.1 %all_gather.28 = bf16[512,768]{1,0:T(8,128)(2,1)} all-gather(bf16[128,768]{1,0:T(8,128)(2,1)} %param.35), channel_id=1, replica_groups=mesh['wide'=8,'narrow'=4] {'narrow'}, dimensions={0}, use_global_device_ids=true | all-gather | bytes 983040 | tf_op jit(solution)/shard_map/all_gather | solution.py:30
  132.3 13.6 %reduce-scatter.13.cloned.1.call-done = bf16[128,768]{1,0:T(8,128)(2,1)} async-done(((bf16[512,768]{1,0:T(8,128)(2,1)}), bf16[128,768]{1,0:T(8,128)(2,1)}) %reduce-scatter.13.cloned.1.call-update) | async-done | bytes 196624 | tf_op jit(solution)/shard_map/reduce_scatter | solution.py:38
  148.0 8.7 all_gather.27
  156.8 10.9 %multiply_convert_fusion.2 = (bf16[512,768]{1,0:T(8,128)(2,1)}, f32[512,768]{1,0:T(8,128)S(1)}, f32[512,768]{1,0:T(8,128)S(1)}) fusion(f32[768]{0:T(1024)S(1)} %copy-done.119, bf16[512,768]{1,0:T(8,128)(2,1)S(1)} %all_gather.27, bf16[2,768,768]{2,1,0:T(8,128)(2,1)S(1)} %copy-done.133), kind=kOutput, calls=%fused_computation.19 | convolution fusion | flops 629932032 | bytes 5902336 | tf_op jit(solution)/shard_map/dot_general | solution.py:179
  167.7 1.8 fusion.132
  172.1 3.2 convolution_convert_fusion.2
  176.2 19.7 %reduce-scatter.17.cloned.1.call-done = bf16[128,768]{1,0:T(8,128)(2,1)} async-done(((bf16[512,768]{1,0:T(8,128)(2,1)}), bf16[128,768]{1,0:T(8,128)(2,1)}) %reduce-scatter.17.cloned.1.call-update) | async-done | bytes 196624 | tf_op jit(solution)/shard_map/reduce_scatter | solution.py:51
  195.9 1.9 fusion.64
  198.9 22.7 %reduce-scatter.15.cloned.1.call-done = bf16[128,768]{1,0:T(8,128)(2,1)} async-done(((bf16[512,768]{1,0:T(8,128)(2,1)}), bf16[128,768]{1,0:T(8,128)(2,1)}) %reduce-scatter.15.cloned.1.call-update) | async-done | bytes 196624 | tf_op jit(solution)/shard_map/reduce_scatter | solution.py:38
  221.6 2.2 fusion.122
  224.6 8.2 all_gather.29
  236.5 2.7 convert_reduce_fusion.5
  245.3 23.8 %reduce-scatter.19.cloned.1.call-done = bf16[128,768]{1,0:T(8,128)(2,1)} async-done(((bf16[512,768]{1,0:T(8,128)(2,1)}), bf16[128,768]{1,0:T(8,128)(2,1)}) %reduce-scatter.19.cloned.1.call-update) | async-done | bytes 196624 | tf_op jit(solution)/shard_map/reduce_scatter | solution.py:51
  269.1 1.8 convert_reduce_fusion.2
  271.5 1.8 fusion.65
  273.3 2.2 convert_reduce_fusion.4
  276.2 8.4 all_gather.30
  284.6 3.5 fusion.133
  290.9 3.6 convolution_bitcast_fusion.2
  294.5 20.1 %reduce-scatter.21.cloned.1.call-done = bf16[128,768]{1,0:T(8,128)(2,1)} async-done(((bf16[512,768]{1,0:T(8,128)(2,1)}), bf16[128,768]{1,0:T(8,128)(2,1)}) %reduce-scatter.21.cloned.1.call-update) | async-done | bytes 196624 | tf_op jit(solution)/shard_map/reduce_scatter | solution.py:51
  314.6 1.7 convert_reduce_fusion.1
  316.4 1.8 fusion.66
  318.2 1.9 fusion.121
  320.1 8.2 all_gather.31
  336.0 1.7 convolution_convert_fusion.4
  337.8 3.4 convolution_bitcast_fusion
  342.7 1.9 fusion.137
  344.7 2.2 convolution_bitcast_fusion.3
  346.9 2.2 convolution_bitcast_fusion.1
  350.6 1.9 fusion.136
  356.1 38.3 %all-reduce.2 = (f32[1,2,192]{2,1,0:T(2,128)S(1)}, f32[1,2,192]{2,1,0:T(2,128)S(1)}, f32[1,768]{1,0:T(1,128)S(1)}, f32[1,768]{1,0:T(1,128)S(1)}) all-reduce(f32[1,2,192]{2,1,0:T(2,128)S(1)} %maximum_bitcast_fusion.5, f32[1,2,192]{2,1,0:T(2,128)S(1)} %maximum_bitcast_fusion.4, ...), channel_id=1, replica_groups=mesh['wide'=8,'narrow'=4] {'wide'}, use_global_device_ids=true, to_apply=%region_56.57 | all-reduce | flops 2304 | bytes 18432 | tf_op jit(solution)/shard_map/psum | solution.py:302
  399.7 1.8 select_reduce_fusion.2
  405.3 43.3 %all-reduce = (f32[2,768]{1,0:T(2,128)}, f32[768]{0:T(1024)}, f32[2,2,768]{2,1,0:T(2,128)}, f32[2,2,768]{2,1,0:T(2,128)}, f32[2,768]{1,0:T(2,128)}, /*index=5*/f32[2,768]{1,0:T(2,128)}) all-reduce(f32[2,768]{1,0:T(2,128)S(1)} %pad_maximum_fusion.9, ...), channel_id=1, replica_groups=mesh['wide'=8,'narrow'=4] {'wide','narrow'}, use_global_device_ids=true, to_apply=%region_34.35 | all-reduce | flops 11520 | bytes 92160 | tf_op jit(solution)/shard_map/psum | solution.py:350
  449.8 363.5 %all-reduce.9.cloned.1.call-done = (f32[1,3,768,192]{2,3,1,0:T(8,128)}, f32[1,3,768,192]{2,3,1,0:T(8,128)}, f32[1,192,768]{2,1,0:T(8,128)}, f32[1,192,768]{2,1,0...) async-done(((f32[1,3,768,192]{2,3,1,0:T(8,128)}, f32[1,3,768,192]{2,3,1,0:T(8,128)}, ...) | async-done | bytes 14155792 | tf_op jit(solution)/shard_map/psum | solution.py:302
  813.3 2.5 pad_maximum_fusion.3
  815.8 3.7 pad_maximum_fusion.2
  819.5 2.7 pad_maximum_fusion
  823.6 2.5 pad_maximum_fusion.1
  826.1 127.5 %all-reduce.7.cloned.1.call-done = (f32[2,256,768]{2,1,0:T(8,128)}, f32[256,768]{1,0:T(8,128)}) async-done(((f32[2,256,768]{2,1,0:T(8,128)}, f32[256,768]{1,0:T(8,128)}), (f32[2,256,768]{2,1,0:T(8,128)}, f32[256,768]{1,0:T(8,128)})) %all-reduce.7.cloned.1.call-update) | async-done | bytes 2359312 | tf_op jit(solution)/shard_map/psum | solution.py:350
  953.6 2.7 copy.210
  (451 shorter events, 80.1 us)
Async XLA Ops:
  7.2 48.4 %reduce-scatter.9.cloned.1.call-start = ((), (), s32[]{:S(2)}) async-start(), calls=%async_computation.8 | async-start | bytes 983040 | tf_op jit(solution)/shard_map/reduce_scatter | solution.py:38
  13.7 11.6 %copy-start.29 = (bf16[2,3,768,192]{2,3,1,0:T(8,128)(2,1)S(1)}, bf16[2,3,768,192]{2,3,1,0:T(8,128)(2,1)}, u32[]{:S(2)}) copy-start(bf16[2,3,768,192]{2,3,1,0:T(8,128)(2,1)} %param.27) | copy-start | bytes 5308420
  14.2 12.3 %copy-start.88 = (f32[128]{0:T(128)}, f32[128]{0:T(128)S(1)}, u32[]{:S(2)}) copy-start(f32[128]{0:T(128)S(1)} %broadcast_multiply_fusion.3) | copy-start | bytes 1540
  14.4 12.0 %copy-start.111 = (f32[128]{0:T(128)}, f32[128]{0:T(128)S(1)}, u32[]{:S(2)}) copy-start(f32[128]{0:T(128)S(1)} %fusion.108) | copy-start | bytes 1540
  15.1 83.5 %copy-start.61 = (f32[768]{0:T(1024)}, f32[768]{0:T(1024)S(1)}, u32[]{:S(2)}) copy-start(f32[768]{0:T(1024)S(1)} %get-tuple-element.218) | copy-start | bytes 9220
  31.3 65.9 %reduce-scatter.11.cloned.1.call-start = ((), (), s32[]{:S(2)}) async-start(), calls=%async_computation.9 | async-start | bytes 983040 | tf_op jit(solution)/shard_map/reduce_scatter | solution.py:38
  55.6 9.8 %copy-start.132 = (bf16[2,768,768]{2,1,0:T(8,128)(2,1)S(1)}, bf16[2,768,768]{2,1,0:T(8,128)(2,1)}, u32[]{:S(2)}) copy-start(bf16[2,768,768]{2,1,0:T(8,128)(2,1)} %param.31) | copy-start | bytes 7077892
  56.8 14.0 %copy-start.90 = (f32[128]{0:T(128)}, f32[128]{0:T(128)S(1)}, u32[]{:S(2)}) copy-start(f32[128]{0:T(128)S(1)} %broadcast_multiply_fusion.2) | copy-start | bytes 1540
  57.0 13.8 %copy-start.125 = (f32[128]{0:T(128)}, f32[128]{0:T(128)S(1)}, u32[]{:S(2)}) copy-start(f32[128]{0:T(128)S(1)} %multiply_reduce_fusion.4) | copy-start | bytes 1540
  57.0 13.8 %copy-start.113 = (f32[128]{0:T(128)}, f32[128]{0:T(128)S(1)}, u32[]{:S(2)}) copy-start(f32[128]{0:T(128)S(1)} %fusion.109) | copy-start | bytes 1540
  65.4 6.3 copy-start.129
  73.4 72.5 %reduce-scatter.13.cloned.1.call-start = ((), (), s32[]{:S(2)}) async-start(), calls=%async_computation.10 | async-start | bytes 983040 | tf_op jit(solution)/shard_map/reduce_scatter | solution.py:38
  97.2 10.6 %copy-start.11 = (bf16[1,3,768,192]{2,3,1,0:T(8,128)(2,1)S(1)}, bf16[1,3,768,192]{2,3,1,0:T(8,128)(2,1)}, u32[]{:S(2)}) copy-start(bf16[1,3,768,192]{2,3,1,0:T(8,128)(2,1)} %get-tuple-element.179) | copy-start | bytes 2654212
  98.4 8.6 copy-start.92
  98.6 8.4 copy-start.127
  98.6 8.4 copy-start.115
  122.1 25.8 %copy-start.66 = (f32[768]{0:T(1024)S(1)}, f32[768]{0:T(1024)}, u32[]{:S(2)}) copy-start(f32[768]{0:T(1024)} %get-tuple-element.221) | copy-start | bytes 9220
  122.1 25.8 %copy-start.75 = (f32[768]{0:T(1024)S(1)}, f32[768]{0:T(1024)}, u32[]{:S(2)}) copy-start(f32[768]{0:T(1024)} %get-tuple-element.130) | copy-start | bytes 9220
  122.1 73.8 %reduce-scatter.17.cloned.1.call-start = ((), (), s32[]{:S(2)}) async-start(), calls=%async_computation.12 | async-start | bytes 983040 | tf_op jit(solution)/shard_map/reduce_scatter | solution.py:51
  145.9 10.8 %copy-start.119 = (f32[768]{0:T(1024)S(1)}, f32[768]{0:T(1024)}, u32[]{:S(2)}) copy-start(f32[768]{0:T(1024)} %get-tuple-element.136) | copy-start | bytes 9220
  145.9 10.8 %copy-start.133 = (bf16[2,768,768]{2,1,0:T(8,128)(2,1)S(1)}, bf16[2,768,768]{2,1,0:T(8,128)(2,1)}, u32[]{:S(2)}) copy-start(bf16[2,768,768]{2,1,0:T(8,128)(2,1)} %param.31) | copy-start | bytes 7077892
  147.2 9.6 copy-start.110
  147.4 9.3 copy-start.116
  156.7 11.0 %copy-start.50 = (bf16[512,768]{1,0:T(8,128)(2,1)}, bf16[512,768]{1,0:T(8,128)(2,1)S(1)}, u32[]{:S(2)}) copy-start(bf16[512,768]{1,0:T(8,128)(2,1)S(1)} %all_gather.27) | copy-start | bytes 2359300
  156.7 11.0 %copy-start.48 = (bf16[512,768]{1,0:T(8,128)(2,1)S(1)}, bf16[512,768]{1,0:T(8,128)(2,1)}, u32[]{:S(2)}) copy-start(bf16[512,768]{1,0:T(8,128)(2,1)} %all_gather.28) | copy-start | bytes 2359300
  156.8 11.0 %copy-start.130 = (bf16[2,768,768]{2,1,0:T(8,128)(2,1)S(1)}, bf16[2,768,768]{2,1,0:T(8,128)(2,1)}, u32[]{:S(2)}) copy-start(bf16[2,768,768]{2,1,0:T(8,128)(2,1)} %param.33) | copy-start | bytes 7077892
  172.1 49.5 %reduce-scatter.15.cloned.1.call-start = ((), (), s32[]{:S(2)}) async-start(), calls=%async_computation.11 | async-start | bytes 983040 | tf_op jit(solution)/shard_map/reduce_scatter | solution.py:38
  175.4 93.7 %reduce-scatter.19.cloned.1.call-start = ((), (), s32[]{:S(2)}) async-start(), calls=%async_computation.13 | async-start | bytes 983040 | tf_op jit(solution)/shard_map/reduce_scatter | solution.py:51
  221.6 12.2 %copy-start.55 = (bf16[2,192,768]{2,1,0:T(8,128)(2,1)S(1)}, bf16[2,192,768]{2,1,0:T(8,128)(2,1)}, u32[]{:S(2)}) copy-start(bf16[2,192,768]{2,1,0:T(8,128)(2,1)} %param.29) | copy-start | bytes 1769476
  223.8 9.1 copy-start.122
  243.5 25.5 %copy-start.62 = (f32[768]{0:T(1024)S(1)}, f32[768]{0:T(1024)}, u32[]{:S(2)}) copy-start(f32[768]{0:T(1024)} %copy-done.61) | copy-start | bytes 9220
  243.5 25.5 %copy-start.93 = (f32[128]{0:T(128)S(1)}, f32[128]{0:T(128)}, u32[]{:S(2)}) copy-start(f32[128]{0:T(128)} %copy-done.92) | copy-start | bytes 1540
  245.2 69.4 %reduce-scatter.21.cloned.1.call-start = ((), (), s32[]{:S(2)}) async-start(), calls=%async_computation.14 | async-start | bytes 983040 | tf_op jit(solution)/shard_map/reduce_scatter | solution.py:51
  269.1 15.6 %copy-start.140 = (f32[512,768]{1,0:T(8,128)S(1)}, f32[512,768]{1,0:T(8,128)}, u32[]{:S(2)}) copy-start(f32[512,768]{1,0:T(8,128)} %get-tuple-element.176) | copy-start | bytes 4718596
  273.3 11.3 %copy-start.131 = (bf16[2,768,768]{2,1,0:T(8,128)(2,1)S(1)}, bf16[2,768,768]{2,1,0:T(8,128)(2,1)}, u32[]{:S(2)}) copy-start(bf16[2,768,768]{2,1,0:T(8,128)(2,1)} %param.33) | copy-start | bytes 7077892
  290.8 105.4 %reduce-scatter.23.cloned.1.call-start = ((), (), s32[]{:S(2)}) async-start(), calls=%async_computation.15 | async-start | bytes 983040 | tf_op jit(solution)/shard_map/reduce_scatter | solution.py:51
  290.9 23.7 %copy-start.91 = (f32[128]{0:T(128)S(1)}, f32[128]{0:T(128)}, u32[]{:S(2)}) copy-start(f32[128]{0:T(128)} %copy-done.90) | copy-start | bytes 1540
  290.9 25.5 %copy-start.126 = (f32[128]{0:T(128)S(1)}, f32[128]{0:T(128)}, u32[]{:S(2)}) copy-start(f32[128]{0:T(128)} %copy-done.125) | copy-start | bytes 1540
  290.9 25.5 %copy-start.114 = (f32[128]{0:T(128)S(1)}, f32[128]{0:T(128)}, u32[]{:S(2)}) copy-start(f32[128]{0:T(128)} %copy-done.113) | copy-start | bytes 1540
  318.2 11.0 %copy-start.56 = (bf16[2,192,768]{2,1,0:T(8,128)(2,1)S(1)}, bf16[2,192,768]{2,1,0:T(8,128)(2,1)}, u32[]{:S(2)}) copy-start(bf16[2,192,768]{2,1,0:T(8,128)(2,1)} %param.29) | copy-start | bytes 1769476
  337.8 475.6 %all-reduce.9.cloned.1.call-start = ((), (), s32[]{:S(2)}) async-start(), calls=%async_computation.17 | async-start | bytes 28311552 | tf_op jit(solution)/shard_map/psum | solution.py:302
  352.6 43.5 %copy-start.89 = (f32[128]{0:T(128)S(1)}, f32[128]{0:T(128)}, u32[]{:S(2)}) copy-start(f32[128]{0:T(128)} %copy-done.88) | copy-start | bytes 1540
  352.6 45.3 %copy-start.124 = (f32[128]{0:T(128)S(1)}, f32[128]{0:T(128)}, u32[]{:S(2)}) copy-start(f32[128]{0:T(128)} %copy-done.123) | copy-start | bytes 1540
  352.6 45.3 %copy-start.112 = (f32[128]{0:T(128)S(1)}, f32[128]{0:T(128)}, u32[]{:S(2)}) copy-start(f32[128]{0:T(128)} %copy-done.111) | copy-start | bytes 1540
  352.6 47.1 %copy-start.102 = (pred[128]{0:T(512)(128)(4,1)S(1)}, pred[128]{0:T(512)(128)(4,1)}, u32[]{:S(2)}) copy-start(pred[128]{0:T(512)(128)(4,1)} %copy-done.101) | copy-start | bytes 388
  352.6 47.1 %copy-start.105 = (pred[128]{0:T(512)(128)(4,1)S(1)}, pred[128]{0:T(512)(128)(4,1)}, u32[]{:S(2)}) copy-start(pred[128]{0:T(512)(128)(4,1)} %copy-done.104) | copy-start | bytes 388
  352.7 600.9 %all-reduce.7.cloned.1.call-start = ((), (), s32[]{:S(2)}) async-start(), calls=%async_computation.16 | async-start | bytes 4718592 | tf_op jit(solution)/shard_map/psum | solution.py:350
  404.6 44.4 %copy-start.103 = (pred[128]{0:T(512)(128)(4,1)S(1)}, pred[128]{0:T(512)(128)(4,1)}, u32[]{:S(2)}) copy-start(pred[128]{0:T(512)(128)(4,1)} %copy-done.101) | copy-start | bytes 388
  (103 other events, 181.4 us)
Sparse Core Ops, SparseCore 0:
  31.4 24.1 reduce-scatter.8
  73.5 23.6 reduce-scatter.10
  122.2 23.6 reduce-scatter.12
  172.2 23.6 reduce-scatter.16
  198.3 23.2 reduce-scatter.14
  245.4 23.6 reduce-scatter.18
  290.9 23.6 reduce-scatter.20
  337.9 23.6 reduce-scatter.22
  367.7 445.5 all-reduce.8
  819.3 134.2 all-reduce.6
where the time goes:
time: 973 us; the launch traced here: 964 us
  waiting for transfers between devices  637 us (65%)
  blocking collectives  152 us (16%)
  matrix products  68.6 us (7%)
  other arithmetic  54.3 us (6%)
  local copies, waits for them, and re-layouts  36.1 us (4%)
  between operations  16 us (2%)
    psum x1, waiting for transfers between devices, per_device(): lax.psum((grad_attention, grad_attnbias, grad_combiner, grad_expander, gr...  364 us
    psum x1, waiting for transfers between devices, per_device(): lax.psum((grad_scales, grad_shifts, grad_combbias, grad_redbias, grad_pro...  128 us
    reduce_scatter x4, waiting for transfers between devices, sum_forward(): lax.psum_scatter(term(jnp.int32(0), local_rows * lax.axis_size('narrow'))...  82.4 us
    reduce_scatter x4, waiting for transfers between devices, sum_backward(): lax.psum_scatter(term(jnp.int32(0), local_rows * lax.axis_size('narrow'))...  63.6 us
    psum x1, blocking collectives, per_device(): lax.psum((grad_scales, grad_shifts, grad_combbias, grad_redbias, grad_pro...  43.3 us
    psum x1, blocking collectives, per_device(): lax.psum((grad_attention, grad_attnbias, grad_combiner, grad_expander, gr...  38.3 us
    all_gather x4, blocking collectives, share_rows(): return lax.all_gather(values, 'narrow', axis=0, tiled=True)  35.2 us
    all_gather x4, blocking collectives, share_grads(): return lax.all_gather(values, 'narrow', axis=0, tiled=True)  34.9 us
  transfers between devices with their start and end apart: 10, of which 9 were waited for; matrix products, arithmetic and copies ran while one was open for 5% of the time, Pallas kernels for 0%

commit v1 on v0

--- a/solution.py
+++ b/solution.py
@@ -1,3 +1,4 @@
+import functools
 from functools import partial
 import math
 import jax
@@ -9,6 +10,34 @@
 norm_eps = 1e-06
 
 
+def find_the_columns(mat, axis_tag):
+    block_out = lax.axis_size(axis_tag)
+    known = lax.axis_index(axis_tag)
+    field_out, v_next, mat_out = (block_out, known, mat.shape[0])
+    ready = range(field_out)
+    reached = map(lambda nth: (nth, (nth + 1) % field_out), ready)
+    in_order = list(reached)
+    pieces_in = list(map(lambda nth: (nth, (nth - 1) % field_out), range(field_out)))
+    next_value = jnp.zeros((*mat.shape[:0], field_out * mat_out, *mat.shape[1:]), mat.dtype)
+    next_value = lax.dynamic_update_slice_in_dim(next_value, mat, v_next * mat_out, axis=0)
+    parts_out = carry_in = mat
+    aux = field_out // 2
+    for h in range(1, aux + 1):
+        parts_out = lax.ppermute(parts_out, axis_tag, in_order)
+        next_value = lax.dynamic_update_slice_in_dim(
+            next_value, parts_out, (v_next - h) % field_out * mat_out, axis=0
+        )
+        if h < field_out - aux:
+            carry_in = lax.ppermute(carry_in, axis_tag, pieces_in)
+            next_value = lax.dynamic_update_slice_in_dim(
+                next_value, carry_in, (v_next + h) % field_out * mat_out, axis=0
+            )
+    return next_value
+
+
+settle_stops_all_by_axis = functools.partial(find_the_columns, axis_tag="narrow")
+
+
 def normalize(values, gain, shift):
     center = values - jnp.mean(values, axis=-1, keepdims=True)
     variance = jnp.mean(center * center, axis=-1, keepdims=True)
@@ -27,7 +56,7 @@
 
 
 def share_grads(values):
-    return lax.all_gather(values, "narrow", axis=0, tiled=True)
+    return settle_stops_all_by_axis(values)
 
 
 def sum_forward(source, weight, local_rows):

time: 973 us -> 985 us (1.012)
  waiting for transfers between devices: 637 us -> 675 us
  blocking collectives: 152 us -> 116 us
    all_gather x4 -> x0, blocking collectives: 34.9 us -> none  [share_grads(): return lax.all_gather(values, 'narrow', axis=0, tiled=True)]
    ppermute x0 -> x12, waiting for transfers between devices: none -> 31.5 us  [the longest x8 31.5 us: find_the_columns(): parts_out = lax.ppermute(parts_out, axis_tag, in_order)]
    unnamed x297 -> x279, local copies, waits for them, and re-layouts: 20.8 us -> 18.9 us
  transfers between devices with their start and end apart: 10 -> 22, of which waited for: 9 -> 17; matrix products, arithmetic and copies ran while one was open for 5% -> 5% of each run, Pallas kernels for 0% -> 0%
where the time goes in v1:
time: 985 us; the launch traced here: 976 us
  waiting for transfers between devices  675 us (69%)
  blocking collectives  116 us (12%)
  matrix products  68.2 us (7%)
  other arithmetic  52.5 us (5%)
  local copies, waits for them, and re-layouts  40.7 us (4%)
  between operations  16.1 us (2%)
    psum x1, waiting for transfers between devices, per_device(): lax.psum((grad_attention, grad_attnbias, grad_combiner, grad_expander, gr...  369 us
    psum x1, waiting for transfers between devices, per_device(): lax.psum((grad_scales, grad_shifts, grad_combbias, grad_redbias, grad_pro...  127 us
    reduce_scatter x4, waiting for transfers between devices, sum_forward(): lax.psum_scatter(term(jnp.int32(0), local_rows * lax.axis_size('narrow'))...  80.2 us
    reduce_scatter x4, waiting for transfers between devices, sum_backward(): lax.psum_scatter(term(jnp.int32(0), local_rows * lax.axis_size('narrow'))...  66.7 us
    psum x1, blocking collectives, per_device(): lax.psum((grad_scales, grad_shifts, grad_combbias, grad_redbias, grad_pro...  42.9 us
    psum x1, blocking collectives, per_device(): lax.psum((grad_attention, grad_attnbias, grad_combiner, grad_expander, gr...  38 us
    all_gather x4, blocking collectives, share_rows(): return lax.all_gather(values, 'narrow', axis=0, tiled=True)  35.2 us
    ppermute x8, waiting for transfers between devices, find_the_columns(): parts_out = lax.ppermute(parts_out, axis_tag, in_order)  31.5 us
  transfers between devices with their start and end apart: 22, of which 17 were waited for; matrix products, arithmetic and copies ran while one was open for 5% of the time, Pallas kernels for 0%

profile of v1, /device:TPU:0, one launch (start us, length us, event | category | flops | bytes accessed | tf_op | source)
XLA Modules:
  0.0 976.2 jit_solution(8696004591237231154)
XLA Ops:
  15.2 10.1 %all_gather.12 = bf16[512,768]{1,0:T(8,128)(2,1)S(1)} all-gather(bf16[128,768]{1,0:T(8,128)(2,1)S(1)} %add_convert_fusion.3), channel_id=1, replica_groups=mesh['wide'=8,'narrow'=4] {'narrow'}, dimensions={0}, use_global_device_ids=true | all-gather | bytes 983040 | tf_op jit(solution)/shard_map/all_gather | solution.py:55
  35.5 23.0 %reduce-scatter.9.cloned.1.call-done = bf16[128,768]{1,0:T(8,128)(2,1)} async-done(((bf16[512,768]{1,0:T(8,128)(2,1)}), bf16[128,768]{1,0:T(8,128)(2,1)}) %reduce-scatter.9.cloned.1.call-update) | async-done | bytes 196624 | tf_op jit(solution)/shard_map/reduce_scatter | solution.py:67
  60.1 8.2 all_gather.13
  68.3 5.4 multiply_convert_fusion.3
  77.1 23.1 %reduce-scatter.11.cloned.1.call-done = bf16[128,768]{1,0:T(8,128)(2,1)} async-done(((bf16[512,768]{1,0:T(8,128)(2,1)}), bf16[128,768]{1,0:T(8,128)(2,1)}) %reduce-scatter.11.cloned.1.call-update) | async-done | bytes 196624 | tf_op jit(solution)/shard_map/reduce_scatter | solution.py:67
  102.2 8.2 all_gather.14
  116.4 2.0 fusion.70
  130.9 1.9 collective-permute-done
  136.1 2.1 collective-permute-done.2
  138.9 11.5 %reduce-scatter.13.cloned.1.call-done = bf16[128,768]{1,0:T(8,128)(2,1)} async-done(((bf16[512,768]{1,0:T(8,128)(2,1)}), bf16[128,768]{1,0:T(8,128)(2,1)}) %reduce-scatter.13.cloned.1.call-update) | async-done | bytes 196624 | tf_op jit(solution)/shard_map/reduce_scatter | solution.py:67
  152.5 8.7 all_gather.15
  161.2 10.9 %multiply_convert_fusion.2 = (bf16[512,768]{1,0:T(8,128)(2,1)}, f32[512,768]{1,0:T(8,128)S(1)}, f32[512,768]{1,0:T(8,128)S(1)}) fusion(f32[768]{0:T(1024)S(1)} %copy-done.108, bf16[512,768]{1,0:T(8,128)(2,1)S(1)} %all_gather.15, bf16[2,768,768]{2,1,0:T(8,128)(2,1)S(1)} %copy-done.122), kind=kOutput, calls=%fused_computation.19 | convolution fusion | flops 629932032 | bytes 5902336 | tf_op jit(solution)/shard_map/dot_general | solution.py:208
  172.2 2.9 fusion.134
  177.8 3.2 convolution_convert_fusion.2
  181.0 20.5 %reduce-scatter.17.cloned.1.call-done = bf16[128,768]{1,0:T(8,128)(2,1)} async-done(((bf16[512,768]{1,0:T(8,128)(2,1)}), bf16[128,768]{1,0:T(8,128)(2,1)}) %reduce-scatter.17.cloned.1.call-update) | async-done | bytes 196624 | tf_op jit(solution)/shard_map/reduce_scatter | solution.py:80
  201.5 1.9 fusion.64
  204.6 22.6 %reduce-scatter.15.cloned.1.call-done = bf16[128,768]{1,0:T(8,128)(2,1)} async-done(((bf16[512,768]{1,0:T(8,128)(2,1)}), bf16[128,768]{1,0:T(8,128)(2,1)}) %reduce-scatter.15.cloned.1.call-update) | async-done | bytes 196624 | tf_op jit(solution)/shard_map/reduce_scatter | solution.py:67
  227.2 2.1 fusion.124
  232.0 4.9 collective-permute-done.3
  237.0 5.0 collective-permute-done.5
  245.6 2.7 convert_reduce_fusion.5
  254.4 23.1 %reduce-scatter.19.cloned.1.call-done = bf16[128,768]{1,0:T(8,128)(2,1)} async-done(((bf16[512,768]{1,0:T(8,128)(2,1)}), bf16[128,768]{1,0:T(8,128)(2,1)}) %reduce-scatter.19.cloned.1.call-update) | async-done | bytes 196624 | tf_op jit(solution)/shard_map/reduce_scatter | solution.py:80
  277.5 1.8 convert_reduce_fusion.2
  280.0 1.8 fusion.65
  281.8 2.1 convert_reduce_fusion.4
  286.5 4.9 collective-permute-done.6
  291.6 5.0 collective-permute-done.8
  296.7 1.8 fusion.135
  301.2 23.0 %reduce-scatter.21.cloned.1.call-done = bf16[128,768]{1,0:T(8,128)(2,1)} async-done(((bf16[512,768]{1,0:T(8,128)(2,1)}), bf16[128,768]{1,0:T(8,128)(2,1)}) %reduce-scatter.21.cloned.1.call-update) | async-done | bytes 196624 | tf_op jit(solution)/shard_map/reduce_scatter | solution.py:80
  326.0 1.8 fusion.66
  327.8 2.0 fusion.122
  331.6 2.2 convolution_bitcast_fusion.2
  333.8 2.7 collective-permute-done.9
  336.6 5.0 collective-permute-done.11
  350.3 3.7 convolution_bitcast_fusion
  355.4 1.9 fusion.139
  357.4 2.2 convolution_bitcast_fusion.3
  359.6 2.2 convolution_bitcast_fusion.1
  363.3 1.9 fusion.138
  366.5 38.0 %all-reduce.2 = (f32[1,2,192]{2,1,0:T(2,128)S(1)}, f32[1,2,192]{2,1,0:T(2,128)S(1)}, f32[1,768]{1,0:T(1,128)S(1)}, f32[1,768]{1,0:T(1,128)S(1)}) all-reduce(f32[1,2,192]{2,1,0:T(2,128)S(1)} %maximum_bitcast_fusion.5, f32[1,2,192]{2,1,0:T(2,128)S(1)} %maximum_bitcast_fusion.4, ...), channel_id=1, replica_groups=mesh['wide'=8,'narrow'=4] {'wide'}, use_global_device_ids=true, to_apply=%region_56.57 | all-reduce | flops 2304 | bytes 18432 | tf_op jit(solution)/shard_map/psum | solution.py:331
  412.3 42.9 %all-reduce = (f32[2,768]{1,0:T(2,128)}, f32[768]{0:T(1024)}, f32[2,2,768]{2,1,0:T(2,128)}, f32[2,2,768]{2,1,0:T(2,128)}, f32[2,768]{1,0:T(2,128)}, /*index=5*/f32[2,768]{1,0:T(2,128)}) all-reduce(f32[2,768]{1,0:T(2,128)S(1)} %pad_maximum_fusion.9, ...), channel_id=1, replica_groups=mesh['wide'=8,'narrow'=4] {'wide','narrow'}, use_global_device_ids=true, to_apply=%region_34.35 | all-reduce | flops 11520 | bytes 92160 | tf_op jit(solution)/shard_map/psum | solution.py:379
  456.3 368.9 %all-reduce.9.cloned.1.call-done = (f32[1,3,768,192]{2,3,1,0:T(8,128)}, f32[1,3,768,192]{2,3,1,0:T(8,128)}, f32[1,192,768]{2,1,0:T(8,128)}, f32[1,192,768]{2,1,0...) async-done(((f32[1,3,768,192]{2,3,1,0:T(8,128)}, f32[1,3,768,192]{2,3,1,0:T(8,128)}, ...) | async-done | bytes 14155792 | tf_op jit(solution)/shard_map/psum | solution.py:331
  825.2 2.5 pad_maximum_fusion.3
  827.7 3.8 pad_maximum_fusion.2
  831.5 2.7 pad_maximum_fusion
  835.6 2.5 pad_maximum_fusion.1
  838.1 127.4 %all-reduce.7.cloned.1.call-done = (f32[2,256,768]{2,1,0:T(8,128)}, f32[256,768]{1,0:T(8,128)}) async-done(((f32[2,256,768]{2,1,0:T(8,128)}, f32[256,768]{1,0:T(8,128)}), (f32[2,256,768]{2,1,0:T(8,128)}, f32[256,768]{1,0:T(8,128)})) %all-reduce.7.cloned.1.call-update) | async-done | bytes 2359312 | tf_op jit(solution)/shard_map/psum | solution.py:379
  965.5 2.7 copy.226
  (470 shorter events, 98.6 us)
Async XLA Ops:
  7.2 51.3 %reduce-scatter.9.cloned.1.call-start = ((), (), s32[]{:S(2)}) async-start(), calls=%async_computation.8 | async-start | bytes 983040 | tf_op jit(solution)/shard_map/reduce_scatter | solution.py:67
  13.7 11.6 %copy-start.28 = (bf16[2,3,768,192]{2,3,1,0:T(8,128)(2,1)S(1)}, bf16[2,3,768,192]{2,3,1,0:T(8,128)(2,1)}, u32[]{:S(2)}) copy-start(bf16[2,3,768,192]{2,3,1,0:T(8,128)(2,1)} %param.27) | copy-start | bytes 5308420
  14.2 12.3 %copy-start.84 = (f32[128]{0:T(128)}, f32[128]{0:T(128)S(1)}, u32[]{:S(2)}) copy-start(f32[128]{0:T(128)S(1)} %broadcast_multiply_fusion.3) | copy-start | bytes 1540
  14.4 12.0 %copy-start.100 = (f32[128]{0:T(128)}, f32[128]{0:T(128)S(1)}, u32[]{:S(2)}) copy-start(f32[128]{0:T(128)S(1)} %fusion.109) | copy-start | bytes 1540
  15.1 87.0 %copy-start.59 = (f32[768]{0:T(1024)}, f32[768]{0:T(1024)S(1)}, u32[]{:S(2)}) copy-start(f32[768]{0:T(1024)S(1)} %get-tuple-element.224) | copy-start | bytes 9220
  34.3 65.9 %reduce-scatter.11.cloned.1.call-start = ((), (), s32[]{:S(2)}) async-start(), calls=%async_computation.9 | async-start | bytes 983040 | tf_op jit(solution)/shard_map/reduce_scatter | solution.py:67
  59.7 14.0 %copy-start.86 = (f32[128]{0:T(128)}, f32[128]{0:T(128)S(1)}, u32[]{:S(2)}) copy-start(f32[128]{0:T(128)S(1)} %broadcast_multiply_fusion.2) | copy-start | bytes 1540
  59.9 13.8 %copy-start.114 = (f32[128]{0:T(128)}, f32[128]{0:T(128)S(1)}, u32[]{:S(2)}) copy-start(f32[128]{0:T(128)S(1)} %multiply_reduce_fusion.4) | copy-start | bytes 1540
  60.0 13.8 %copy-start.102 = (f32[128]{0:T(128)}, f32[128]{0:T(128)S(1)}, u32[]{:S(2)}) copy-start(f32[128]{0:T(128)S(1)} %fusion.110) | copy-start | bytes 1540
  76.4 74.0 %reduce-scatter.13.cloned.1.call-start = ((), (), s32[]{:S(2)}) async-start(), calls=%async_computation.10 | async-start | bytes 983040 | tf_op jit(solution)/shard_map/reduce_scatter | solution.py:67
  100.2 11.1 %copy-start.10 = (bf16[1,3,768,192]{2,3,1,0:T(8,128)(2,1)S(1)}, bf16[1,3,768,192]{2,3,1,0:T(8,128)(2,1)}, u32[]{:S(2)}) copy-start(bf16[1,3,768,192]{2,3,1,0:T(8,128)(2,1)} %get-tuple-element.185) | copy-start | bytes 2654212
  126.5 75.0 %reduce-scatter.17.cloned.1.call-start = ((), (), s32[]{:S(2)}) async-start(), calls=%async_computation.12 | async-start | bytes 983040 | tf_op jit(solution)/shard_map/reduce_scatter | solution.py:80
  126.6 6.3 collective-permute-start
  127.0 7.5 collective-permute-start.1
  129.3 23.0 %copy-start.65 = (f32[768]{0:T(1024)S(1)}, f32[768]{0:T(1024)}, u32[]{:S(2)}) copy-start(f32[768]{0:T(1024)} %get-tuple-element.227) | copy-start | bytes 9220
  129.3 23.0 %copy-start.72 = (f32[768]{0:T(1024)S(1)}, f32[768]{0:T(1024)}, u32[]{:S(2)}) copy-start(f32[768]{0:T(1024)} %get-tuple-element.130) | copy-start | bytes 9220
  132.9 5.3 collective-permute-start.2
  177.7 49.5 %reduce-scatter.15.cloned.1.call-start = ((), (), s32[]{:S(2)}) async-start(), calls=%async_computation.11 | async-start | bytes 983040 | tf_op jit(solution)/shard_map/reduce_scatter | solution.py:67
  177.8 49.4 %copy-start.73 = (f32[768]{0:T(1024)S(1)}, f32[768]{0:T(1024)}, u32[]{:S(2)}) copy-start(f32[768]{0:T(1024)} %get-tuple-element.134) | copy-start | bytes 9220
  181.0 96.5 %reduce-scatter.19.cloned.1.call-start = ((), (), s32[]{:S(2)}) async-start(), calls=%async_computation.13 | async-start | bytes 983040 | tf_op jit(solution)/shard_map/reduce_scatter | solution.py:80
  229.3 13.6 %copy-start.53 = (bf16[2,192,768]{2,1,0:T(8,128)(2,1)S(1)}, bf16[2,192,768]{2,1,0:T(8,128)(2,1)}, u32[]{:S(2)}) copy-start(bf16[2,192,768]{2,1,0:T(8,128)(2,1)} %param.29) | copy-start | bytes 1769476
  230.2 6.7 collective-permute-start.3
  230.3 6.6 collective-permute-start.4
  236.9 5.1 collective-permute-start.5
  252.6 24.9 %copy-start.60 = (f32[768]{0:T(1024)S(1)}, f32[768]{0:T(1024)}, u32[]{:S(2)}) copy-start(f32[768]{0:T(1024)} %copy-done.59) | copy-start | bytes 9220
  252.6 24.9 %copy-start.89 = (f32[128]{0:T(128)S(1)}, f32[128]{0:T(128)}, u32[]{:S(2)}) copy-start(f32[128]{0:T(128)} %copy-done.88) | copy-start | bytes 1540
  254.3 69.9 %reduce-scatter.21.cloned.1.call-start = ((), (), s32[]{:S(2)}) async-start(), calls=%async_computation.14 | async-start | bytes 983040 | tf_op jit(solution)/shard_map/reduce_scatter | solution.py:80
  277.5 19.1 %copy-start.131 = (f32[512,768]{1,0:T(8,128)S(1)}, f32[512,768]{1,0:T(8,128)}, u32[]{:S(2)}) copy-start(f32[512,768]{1,0:T(8,128)} %get-tuple-element.204) | copy-start | bytes 4718596
  281.8 14.9 %copy-start.130 = (f32[512,768]{1,0:T(8,128)S(1)}, f32[512,768]{1,0:T(8,128)}, u32[]{:S(2)}) copy-start(f32[512,768]{1,0:T(8,128)} %get-tuple-element.182) | copy-start | bytes 4718596
  283.9 12.8 %copy-start.120 = (bf16[2,768,768]{2,1,0:T(8,128)(2,1)S(1)}, bf16[2,768,768]{2,1,0:T(8,128)(2,1)}, u32[]{:S(2)}) copy-start(bf16[2,768,768]{2,1,0:T(8,128)(2,1)} %param.33) | copy-start | bytes 7077892
  284.7 6.7 collective-permute-start.6
  284.7 6.8 collective-permute-start.7
  291.4 5.2 collective-permute-start.8
  299.3 24.9 %copy-start.87 = (f32[128]{0:T(128)S(1)}, f32[128]{0:T(128)}, u32[]{:S(2)}) copy-start(f32[128]{0:T(128)} %copy-done.86) | copy-start | bytes 1540
  299.3 26.6 %copy-start.115 = (f32[128]{0:T(128)S(1)}, f32[128]{0:T(128)}, u32[]{:S(2)}) copy-start(f32[128]{0:T(128)} %copy-done.114) | copy-start | bytes 1540
  299.3 26.6 %copy-start.103 = (f32[128]{0:T(128)S(1)}, f32[128]{0:T(128)}, u32[]{:S(2)}) copy-start(f32[128]{0:T(128)} %copy-done.102) | copy-start | bytes 1540
  301.1 104.6 %reduce-scatter.23.cloned.1.call-start = ((), (), s32[]{:S(2)}) async-start(), calls=%async_computation.15 | async-start | bytes 983040 | tf_op jit(solution)/shard_map/reduce_scatter | solution.py:80
  329.8 12.7 %copy-start.54 = (bf16[2,192,768]{2,1,0:T(8,128)(2,1)S(1)}, bf16[2,192,768]{2,1,0:T(8,128)(2,1)}, u32[]{:S(2)}) copy-start(bf16[2,192,768]{2,1,0:T(8,128)(2,1)} %param.29) | copy-start | bytes 1769476
  329.8 6.7 collective-permute-start.9
  329.9 6.6 collective-permute-start.10
  336.5 5.1 collective-permute-start.11
  350.3 474.9 %all-reduce.9.cloned.1.call-start = ((), (), s32[]{:S(2)}) async-start(), calls=%async_computation.17 | async-start | bytes 28311552 | tf_op jit(solution)/shard_map/psum | solution.py:331
  365.3 40.4 %copy-start.85 = (f32[128]{0:T(128)S(1)}, f32[128]{0:T(128)}, u32[]{:S(2)}) copy-start(f32[128]{0:T(128)} %copy-done.84) | copy-start | bytes 1540
  365.3 41.5 %copy-start.113 = (f32[128]{0:T(128)S(1)}, f32[128]{0:T(128)}, u32[]{:S(2)}) copy-start(f32[128]{0:T(128)} %copy-done.112) | copy-start | bytes 1540
  365.3 41.5 %copy-start.101 = (f32[128]{0:T(128)S(1)}, f32[128]{0:T(128)}, u32[]{:S(2)}) copy-start(f32[128]{0:T(128)} %copy-done.100) | copy-start | bytes 1540
  365.3 42.8 %copy-start.94 = (pred[128]{0:T(512)(128)(4,1)S(1)}, pred[128]{0:T(512)(128)(4,1)}, u32[]{:S(2)}) copy-start(pred[128]{0:T(512)(128)(4,1)} %copy-done.93) | copy-start | bytes 388
  365.3 42.8 %copy-start.96 = (pred[128]{0:T(512)(128)(4,1)S(1)}, pred[128]{0:T(512)(128)(4,1)}, u32[]{:S(2)}) copy-start(pred[128]{0:T(512)(128)(4,1)} %copy-done.95) | copy-start | bytes 388
  365.4 600.1 %all-reduce.7.cloned.1.call-start = ((), (), s32[]{:S(2)}) async-start(), calls=%async_computation.16 | async-start | bytes 4718592 | tf_op jit(solution)/shard_map/psum | solution.py:379
  (106 other events, 275.6 us)
Sparse Core Ops, SparseCore 0:
  34.4 24.1 reduce-scatter.8
  76.5 23.6 reduce-scatter.10
  126.6 23.6 reduce-scatter.12
  177.9 23.6 reduce-scatter.16
  203.9 23.2 reduce-scatter.14
  254.5 23.0 reduce-scatter.18
  301.2 22.9 reduce-scatter.20
  350.4 23.0 reduce-scatter.22
  379.6 445.5 all-reduce.8
  831.2 134.2 all-reduce.6
